TPU v7x, 32 devices: a whole 2x2x4 slice. The times are simulated.
32 devices in a mesh: dp: 8 (over z, x), seq: 4 (over y, core).
Axes of the slice: x: 2, y: 2, z: 4, core: 2. Of those that a mesh axis runs over, the one named last changes fastest.
Arguments:
- field: bfloat16 [8, 2048, 1024], P('dp', 'seq'), may hold values from -6 to 6
- eq_embed: bfloat16 [8, 512, 1024], P('dp', 'seq'), may hold values from -6 to 6
- eq_len: int32 [8], replicated, may hold values from 1 to 512, 2048 in all
- owner: int32 [8], replicated, may hold values from 0 to 7, as said below
- norm_gain: float32 [1024], replicated, may hold values from 0.1 to 1.9
- w_qkv: bfloat16 [1024, 3072], replicated, may hold values from -0.176776695 to 0.176776695
- w_out: bfloat16 [1024, 1024], replicated, may hold values from -0.1875 to 0.1875
- cross_gain: float32 [1024], replicated, may hold values from 0.1 to 1.9
- w_cq: bfloat16 [1024, 1024], replicated, may hold values from -0.125 to 0.125
- w_ckv: bfloat16 [1024, 2048], replicated, may hold values from -0.125 to 0.125
- w_cout: bfloat16 [1024, 1024], replicated, may hold values from -0.1875 to 0.1875
Outputs:
- joined: bfloat16 [8, 2048, 1024], P('dp', 'seq')
Inputs may be any that keep to these rules, and one draw needn't show every extreme that they name: `owner`: every slot number appears exactly once. `eq_len`: some slot has all 512 tokens real.
All inputs are finite; a program needn't handle non-finite values.
Results may differ from a plain program's by a relative error of at most 0.0055.
Values may be sent and summed in bfloat16 or wider, within the bound.
A program may use at most 128 MiB of HBM per device.

v0:
```python
import jax
import jax.numpy as jnp
from jax import lax
from jax.sharding import PartitionSpec as P

D = 1024
HEADS = 16
HEAD_DIM = 64


def normalize(values, gain):
    return values * lax.rsqrt(jnp.mean(values * values, axis=-1, keepdims=True) + 1e-06) * gain


def attend(query, keys, values, valid):
    rows = query.shape[0]
    heads = query.shape[1]
    depth = query.shape[2]
    block = min(512, rows)
    scale = depth ** (-0.5)

    def one_block(query_block):
        scores = (
            jnp.einsum("qhd,khd->hqk", query_block, keys, preferred_element_type=jnp.float32)
            * scale
        )
        expo = jnp.where(valid[None, None, :], jnp.exp(scores), 0.0)
        weights = (expo / jnp.sum(expo, axis=-1, keepdims=True)).astype(jnp.bfloat16)
        return jnp.einsum(
            "hqk,khd->qhd", weights, values, preferred_element_type=jnp.float32
        ).astype(jnp.bfloat16)

    blocks = lax.map(one_block, query.reshape(rows // block, block, heads, depth))
    return blocks.reshape(rows, heads * depth)


def pick_slot(wanted, carry, piece):
    inside = (wanted >= 0) & (wanted < piece.shape[0])
    picked = lax.dynamic_index_in_dim(
        piece, jnp.clip(wanted, 0, piece.shape[0] - 1), 0, keepdims=False
    )
    return jnp.where(inside, picked, carry)


def per_device(
    field, eq_embed, eq_len, owner, norm_gain, w_qkv, w_out, cross_gain, w_cq, w_ckv, w_cout
):
    tokens = field[0].astype(jnp.float32)
    tok_rows = tokens.shape[0]
    groups = lax.axis_size("seq")
    head_count = HEADS // groups
    normed = normalize(tokens, norm_gain).astype(jnp.bfloat16)
    projected = jnp.dot(normed, w_qkv, preferred_element_type=jnp.float32).astype(jnp.bfloat16)
    stacked = projected.reshape(tok_rows, 3, D)
    local_heads = lax.all_to_all(stacked, "seq", split_axis=2, concat_axis=0, tiled=True)
    seq_rows = local_heads.shape[0]
    split = local_heads.reshape(seq_rows, 3, head_count, HEAD_DIM)
    every = jnp.ones((seq_rows,), dtype=bool)
    attended = attend(split[:, 0], split[:, 1], split[:, 2], every)
    merged = lax.all_to_all(attended, "seq", split_axis=0, concat_axis=1, tiled=True)
    mixed = tokens + jnp.dot(merged, w_out, preferred_element_type=jnp.float32)
    cross_in = normalize(mixed, cross_gain).astype(jnp.bfloat16)
    cross_q = jnp.dot(cross_in, w_cq, preferred_element_type=jnp.float32).astype(jnp.bfloat16)
    slot = lax.dynamic_index_in_dim(owner, lax.axis_index("dp"), 0, keepdims=False)
    length = lax.dynamic_index_in_dim(eq_len, slot, 0, keepdims=False)
    eq_rows = eq_embed.shape[1]
    empty = jnp.zeros(eq_embed.shape[1:], jnp.bfloat16)
    owned_rows = pick_slot(slot, empty, lax.all_gather(eq_embed, "dp", axis=0, tiled=True))
    owned_kv = jnp.dot(owned_rows, w_ckv, preferred_element_type=jnp.float32).astype(jnp.bfloat16)
    whole_kv = lax.all_gather(owned_kv, "seq", axis=0, tiled=True)
    whole_kv = whole_kv.reshape(eq_rows * groups, 2, HEADS, HEAD_DIM)
    valid = jnp.arange(eq_rows * groups, dtype=jnp.int32) < length
    cross_att = attend(
        cross_q.reshape(tok_rows, HEADS, HEAD_DIM), whole_kv[:, 0], whole_kv[:, 1], valid
    )
    joined = mixed + jnp.dot(cross_att, w_cout, preferred_element_type=jnp.float32)
    return joined.astype(jnp.bfloat16)[None]


def solution(mesh):
    in_specs = (
        P("dp", "seq", None),
        P("dp", "seq", None),
        P(),
        P(),
        P(),
        P(),
        P(),
        P(),
        P(),
        P(),
        P(),
    )
    out_specs = P("dp", "seq", None)
    return jax.shard_map(
        per_device, mesh=mesh, in_specs=in_specs, out_specs=out_specs, check_vma=False
    )
```

profile of v0, /device:TPU:0, one launch (start us, length us, event | category | flops | bytes accessed | tf_op | source)
XLA Modules:
  0.0 189.4 jit_solution(14081409868850262506)
XLA Ops:
  6.5 0.0 copy-start
  6.5 0.0 all-gather.3.cloned.1.call-start
  6.5 0.7 all-gather.3.cloned.1.call-update
  7.3 1.5 fusion.12
  8.8 8.3 %convolution_convert_fusion = bf16[512,3072]{1,0:T(8,128)(2,1)} fusion(bf16[1024,3072]{1,0:T(8,128)(2,1)} %param.18, bf16[1,512,1024]{2,1,0:T(8,128)(2,1)} %param.13, f32[1024]{0:T(1024)} %param.17, f32[512]{0:T(512)S(1)} %add_rsqrt_fusion.1), kind=kOutput, calls=%fused_computation.16 | convolution fusion | flops 3224895488 | bytes 10491904 | tf_op jit(solution)/shard_map/dot_general | solution.py:53
  17.1 4.7 %copy.28 = bf16[512,3072]{0,1:T(8,128)(2,1)} copy(bf16[512,3072]{1,0:T(8,128)(2,1)} %convolution_convert_fusion) | data formatting | bytes 6291456 | tf_op jit(solution)/shard_map/convert_element_type | solution.py:53
  21.7 6.5 %copy.29 = bf16[512,3,1024]{0,1,2:T(4,128)(2,1)} copy(bf16[512,3,1024]{0,2,1:T(8,128)(2,1)} %bitcast.75) | data formatting | bytes 6291456 | tf_op jit(solution)/shard_map/reshape | solution.py:54
  28.3 5.0 %all-to-all-start = ((bf16[512,3,1024]{0,1,2:T(4,128)(2,1)}), bf16[512,3,1024]{0,1,2:T(4,128)(2,1)}, u32[]{:S(2)}, u32[]{:S(2)}) async-start(bf16[512,3,1024]{0,1,2:T(4,128)(2,1)} %copy.29), calls=%async_computation | async-start | bytes 8388608 | tf_op jit(solution)/shard_map/all_to_all | solution.py:55
  33.3 0.2 all-gather.5.cloned.1.call-start
  33.5 0.0 copy-done.8
  33.5 0.6 dynamic_slice.18
  35.8 46.4 %all-to-all-done = bf16[512,3,1024]{0,1,2:T(4,128)(2,1)} async-done(((bf16[512,3,1024]{0,1,2:T(4,128)(2,1)}), bf16[512,3,1024]{0,1,2:T(4,128)(2,1)}, u32[]{:S(2)}, u32[]{:S(2)}) %all-to-all-start) | async-done | bytes 3145760 | tf_op jit(solution)/shard_map/all_to_all | solution.py:55
  82.2 3.0 %copy.30 = bf16[512,3,1024]{0,2,1:T(8,128)(2,1)S(1)} copy(bf16[512,3,1024]{0,1,2:T(4,128)(2,1)} %all-to-all-done) | data formatting | bytes 6291456 | tf_op jit(solution)/shard_map/all_to_all | solution.py:55
  85.1 4.1 %copy.31 = bf16[4,512,3,256]{1,0,3,2:T(4,128)(2,1)} copy(bf16[4,512,3,256]{1,3,0,2:T(8,128)(2,1)S(1)} %bitcast.76) | data formatting | bytes 6291456 | tf_op jit(solution)/shard_map/all_to_all | solution.py:55
  89.2 6.1 %reshape.50 = bf16[2048,3,4,64]{0,3,2,1:T(8,128)(2,1)} reshape(bf16[4,512,3,256]{1,0,3,2:T(4,128)(2,1)} %copy.31) | data formatting | bytes 6291456 | tf_op jit(solution)/shard_map/reshape | solution.py:57
  95.3 3.6 %slice_bitcast_fusion.4 = (bf16[2048,4,64]{0,2,1:T(8,128)(2,1)}, bf16[2048,4,64]{0,2,1:T(8,128)(2,1)S(1)}, bf16[2048,1,4,64]{0,3,2,1:T(8,128)(2,1)}) fusion(bf16[2048,3,4,64]{0,3,2,1:T(8,128)(2,1)} %reshape.50), kind=kLoop, calls=%fused_computation.33 | loop fusion | bytes 6291456 | tf_op jit(solution)/shard_map/squeeze | solution.py:59
  98.9 2.6 %reshape_squeeze.3 = bf16[4,512,4,64]{1,0,3,2:T(4,128)(2,1)} reshape(bf16[2048,1,4,64]{0,3,2,1:T(8,128)(2,1)} %get-tuple-element.80) | data formatting | bytes 2097152 | tf_op jit(solution)/shard_map/reshape;squeeze | solution.py:33
  101.5 2.4 %copy.32 = bf16[4,512,4,64]{1,3,2,0:T(8,128)(2,1)} copy(bf16[4,512,4,64]{1,0,3,2:T(4,128)(2,1)} %reshape_squeeze.3) | data formatting | bytes 2097152 | tf_op jit(solution)/shard_map/while | solution.py:33
  103.9 3.8 %convolution_convert_fusion.1 = bf16[128,2048]{1,0:T(8,128)(2,1)} fusion(bf16[1024,2048]{1,0:T(8,128)(2,1)} %param.22, bf16[8,128,1024]{2,1,0:T(8,128)(2,1)} %all-gather.3.cloned.1.call-done, s32[]{:T(128)S(6)} %min.4, pred[]{:T(512)S(6)} %and.4), kind=kOutput, calls=%fused_computation.20 | convolution fusion | flops 537264128 | bytes 4980741 | tf_op jit(solution)/shard_map/dot_general | solution.py:69
  107.7 0.0 all-gather.5.cloned.1.call-update
  107.8 0.0 copy-start.9
  107.8 33.5 %while.2 = (s32[]{:T(128)}, bf16[4,512,4,64]{1,3,2,0:T(8,128)(2,1)}, bf16[4,512,4,64]{1,3,2,0:T(8,128)(2,1)}, bf16[2048,4,64]{0,2,1:T(8,128)(2,1)S(1)}, bf16[2048,4,64]{0,2,1:T(8,128)(2,1)}, /*index=5*/s32[]{:T(128)}) while((s32[]{:T(128)}, bf16[4,512,4,64]{1,3,2,0:T(8,128)(2,1)}, bf16[4,512,4,64]{1,3,2,0:T(8,128)(2,1)}, ...), condition=%wide.region_3.4_spmd, body=%wide.region_1.3_spmd.sunk | while | flops 1094842368 | bytes 40386672 | solution.py:33
  107.8 0.0 copy-start.4
  107.8 4.0 %fusion.49 = (f32[4,512]{1,0:T(4,128)S(1)}, f32[4,512,2048]{2,1,0:T(8,128)S(1)}) fusion(bf16[2048,4,64]{0,2,1:T(8,128)(2,1)S(1)} %get-tuple-element.135, bf16[4,512,4,64]{1,3,2,0:T(8,128)(2,1)} %get-tuple-element.134, s32[]{:T(128)S(6)} %copy.40), kind=kOutput, calls=%fused_computation.2.clone.1 | convolution fusion | flops 545257472 | bytes 18096132 | tf_op jit(solution)/shard_map/while/body/eval_jaxpr/qhd,khd->hqk/dot_general | solution.py:24
  111.8 0.0 copy-done.4
  111.9 4.3 %fusion.50 = bf16[4,512,4,64]{1,3,2,0:T(8,128)(2,1)} fusion(bf16[4,512,4,64]{1,3,2,0:T(8,128)(2,1)} %get-tuple-element.127, s32[]{:T(128)S(6)} %copy.40, bf16[2048,4,64]{0,2,1:T(8,128)(2,1)S(1)} %copy-done.4, f32[4,512,2048]{2,1,0:T(8,128)S(1)} %get-tuple-element.118, f32[4,512]{1,0:T(4,128)S(1)} %get-tuple-element.119), kind=kOutput, calls=%fused_computation.6.clone.1 | convolution fusion | flops 549584896 | bytes 18096132 | tf_op jit(solution)/shard_map/while/body/eval_jaxpr/hqk,khd->qhd/dot_general | solution.py:29
  116.2 4.1 %fusion.49 = (f32[4,512]{1,0:T(4,128)S(1)}, f32[4,512,2048]{2,1,0:T(8,128)S(1)}) fusion(bf16[2048,4,64]{0,2,1:T(8,128)(2,1)S(1)} %get-tuple-element.135, bf16[4,512,4,64]{1,3,2,0:T(8,128)(2,1)} %get-tuple-element.134, s32[]{:T(128)S(6)} %copy.40), kind=kOutput, calls=%fused_computation.2.clone.1 | convolution fusion | flops 545257472 | bytes 18096132 | tf_op jit(solution)/shard_map/while/body/eval_jaxpr/qhd,khd->hqk/dot_general | solution.py:24
  120.3 0.0 copy-done.4
  120.3 4.3 %fusion.50 = bf16[4,512,4,64]{1,3,2,0:T(8,128)(2,1)} fusion(bf16[4,512,4,64]{1,3,2,0:T(8,128)(2,1)} %get-tuple-element.127, s32[]{:T(128)S(6)} %copy.40, bf16[2048,4,64]{0,2,1:T(8,128)(2,1)S(1)} %copy-done.4, f32[4,512,2048]{2,1,0:T(8,128)S(1)} %get-tuple-element.118, f32[4,512]{1,0:T(4,128)S(1)} %get-tuple-element.119), kind=kOutput, calls=%fused_computation.6.clone.1 | convolution fusion | flops 549584896 | bytes 18096132 | tf_op jit(solution)/shard_map/while/body/eval_jaxpr/hqk,khd->qhd/dot_general | solution.py:29
  124.6 4.0 %fusion.49 = (f32[4,512]{1,0:T(4,128)S(1)}, f32[4,512,2048]{2,1,0:T(8,128)S(1)}) fusion(bf16[2048,4,64]{0,2,1:T(8,128)(2,1)S(1)} %get-tuple-element.135, bf16[4,512,4,64]{1,3,2,0:T(8,128)(2,1)} %get-tuple-element.134, s32[]{:T(128)S(6)} %copy.40), kind=kOutput, calls=%fused_computation.2.clone.1 | convolution fusion | flops 545257472 | bytes 18096132 | tf_op jit(solution)/shard_map/while/body/eval_jaxpr/qhd,khd->hqk/dot_general | solution.py:24
  128.6 4.3 %fusion.50 = bf16[4,512,4,64]{1,3,2,0:T(8,128)(2,1)} fusion(bf16[4,512,4,64]{1,3,2,0:T(8,128)(2,1)} %get-tuple-element.127, s32[]{:T(128)S(6)} %copy.40, bf16[2048,4,64]{0,2,1:T(8,128)(2,1)S(1)} %copy-done.4, f32[4,512,2048]{2,1,0:T(8,128)S(1)} %get-tuple-element.118, f32[4,512]{1,0:T(4,128)S(1)} %get-tuple-element.119), kind=kOutput, calls=%fused_computation.6.clone.1 | convolution fusion | flops 549584896 | bytes 18096132 | tf_op jit(solution)/shard_map/while/body/eval_jaxpr/hqk,khd->qhd/dot_general | solution.py:29
  132.9 4.0 %fusion.49 = (f32[4,512]{1,0:T(4,128)S(1)}, f32[4,512,2048]{2,1,0:T(8,128)S(1)}) fusion(bf16[2048,4,64]{0,2,1:T(8,128)(2,1)S(1)} %get-tuple-element.135, bf16[4,512,4,64]{1,3,2,0:T(8,128)(2,1)} %get-tuple-element.134, s32[]{:T(128)S(6)} %copy.40), kind=kOutput, calls=%fused_computation.2.clone.1 | convolution fusion | flops 545257472 | bytes 18096132 | tf_op jit(solution)/shard_map/while/body/eval_jaxpr/qhd,khd->hqk/dot_general | solution.py:24
  137.0 0.0 copy-done.4
  137.0 4.3 %fusion.50 = bf16[4,512,4,64]{1,3,2,0:T(8,128)(2,1)} fusion(bf16[4,512,4,64]{1,3,2,0:T(8,128)(2,1)} %get-tuple-element.127, s32[]{:T(128)S(6)} %copy.40, bf16[2048,4,64]{0,2,1:T(8,128)(2,1)S(1)} %copy-done.4, f32[4,512,2048]{2,1,0:T(8,128)S(1)} %get-tuple-element.118, f32[4,512]{1,0:T(4,128)S(1)} %get-tuple-element.119), kind=kOutput, calls=%fused_computation.6.clone.1 | convolution fusion | flops 549584896 | bytes 18096132 | tf_op jit(solution)/shard_map/while/body/eval_jaxpr/hqk,khd->qhd/dot_general | solution.py:29
  141.3 3.7 %all-to-all-start.1 = ((bf16[4,512,256]{1,2,0:T(8,128)(2,1)}), bf16[4,512,256]{1,2,0:T(8,128)(2,1)S(1)}, u32[]{:S(2)}, u32[]{:S(2)}) async-start(bf16[4,512,256]{1,2,0:T(8,128)(2,1)} %bitcast.80), calls=%async_computation.1 | async-start | bytes 2097152 | tf_op jit(solution)/shard_map/all_to_all | solution.py:60
  146.7 0.6 dynamic_slice.20
  147.3 0.6 iota_compare_fusion
  148.0 11.3 %all-to-all-done.1 = bf16[4,512,256]{1,2,0:T(8,128)(2,1)S(1)} async-done(((bf16[4,512,256]{1,2,0:T(8,128)(2,1)}), bf16[4,512,256]{1,2,0:T(8,128)(2,1)S(1)}, u32[]{:S(2)}, u32[]{:S(2)}) %all-to-all-start.1) | async-done | bytes 1048608 | tf_op jit(solution)/shard_map/all_to_all | solution.py:60
  159.2 2.7 %multiply_reduce_fusion = (f32[512]{0:T(512)S(1)}, f32[512,1024]{1,0:T(8,128)S(1)}) fusion(bf16[512,1024]{0,1:T(8,128)(2,1)S(1)} %bitcast.77, bf16[1024,1024]{1,0:T(8,128)(2,1)S(1)} %copy-done, bf16[1,512,1024]{2,1,0:T(8,128)(2,1)} %param.13), kind=kOutput, calls=%fused_computation.26 | convolution fusion | flops 1075838464 | bytes 6293504 | tf_op jit(solution)/shard_map/dot_general | solution.py:61
  162.0 1.3 copy-done.1
  163.3 2.3 %convolution_convert_fusion.2 = bf16[512,1024]{1,0:T(8,128)(2,1)} fusion(bf16[1024,1024]{1,0:T(8,128)(2,1)S(1)} %copy-done.5, f32[512,1024]{1,0:T(8,128)S(1)} %get-tuple-element.82, f32[1024]{0:T(1024)S(1)} %copy-done.7, f32[512]{0:T(512)S(1)} %add_rsqrt_fusion), kind=kOutput, calls=%fused_computation.28 | convolution fusion | flops 1075838976 | bytes 5249024 | tf_op jit(solution)/shard_map/dot_general | solution.py:63
  165.6 1.5 copy.34
  167.1 0.0 all-gather.5.cloned.1.call-done
  167.1 3.9 %copy.33 = bf16[512,2048]{0,1:T(8,128)(2,1)} copy(bf16[512,2048]{1,0:T(8,128)(2,1)} %all-gather.5.cloned.1.call-done) | data formatting | bytes 4194304 | tf_op jit(solution)/shard_map/all_gather | solution.py:70
  171.0 5.5 %fusion.10 = (f32[16,512]{1,0:T(8,128)S(1)}, f32[16,512,512]{1,2,0:T(8,128)S(1)}) fusion(pred[512]{0:T(512)(128)(4,1)S(1)} %iota_compare_fusion, bf16[512,16,64]{0,2,1:T(8,128)(2,1)S(1)} %bitcast.81, bf16[512,2,16,64]{0,3,2,1:T(8,128)(2,1)} %bitcast.78), kind=kOutput, calls=%fused_computation.14 | convolution fusion | flops 549445632 | bytes 18907648 | tf_op jit(solution)/shard_map/while/body/eval_jaxpr/qhd,khd->hqk/dot_general | solution.py:24
  176.6 0.0 copy-start.6
  176.6 3.7 %fusion.15 = bf16[16,64,512]{2,1,0:T(8,128)(2,1)S(1)} fusion(f32[16,512,512]{1,2,0:T(8,128)S(1)} %get-tuple-element.84, f32[16,512]{1,0:T(8,128)S(1)} %get-tuple-element.83, pred[512]{0:T(512)(128)(4,1)S(1)} %iota_compare_fusion, bf16[512,2,16,64]{0,3,2,1:T(8,128)(2,1)S(1)} %bitcast.79), kind=kOutput, calls=%fused_computation.27 | convolution fusion | flops 554172416 | bytes 18907648 | tf_op jit(solution)/shard_map/while/body/eval_jaxpr/hqk,khd->qhd/dot_general | solution.py:29
  180.4 2.2 %fusion.16 = bf16[1,512,1024]{2,1,0:T(8,128)(2,1)} fusion(f32[512,1024]{1,0:T(8,128)S(1)} %copy-done.2, bf16[512,1024]{0,1:T(8,128)(2,1)S(1)} %bitcast.82, bf16[1024,1024]{1,0:T(8,128)(2,1)S(1)} %copy-done.6), kind=kOutput, calls=%fused_computation.29 | convolution fusion | flops 1074790400 | bytes 6291456 | tf_op jit(solution)/shard_map/dot_general | solution.py:76
  (21 shorter events, 0.0 us)
Async XLA Ops:
  6.5 152.7 %copy-start = (bf16[1024,1024]{1,0:T(8,128)(2,1)S(1)}, bf16[1024,1024]{1,0:T(8,128)(2,1)}, u32[]{:S(2)}) copy-start(bf16[1024,1024]{1,0:T(8,128)(2,1)} %param.19) | copy-start | bytes 6291460
  6.5 97.4 %all-gather.3.cloned.1.call-start = ((), (), s32[]{:S(2)}) async-start(), calls=%async_computation.2 | async-start | bytes 2359296 | tf_op jit(solution)/shard_map/all_gather | solution.py:68
  28.3 5.2 %copy-start.8 = (s32[8]{0:T(128)S(1)}, s32[8]{0:T(128)}, u32[]{:S(2)}) copy-start(s32[8]{0:T(128)} %param.16) | copy-start | bytes 100
  28.3 53.9 %all-to-all-start = ((bf16[512,3,1024]{0,1,2:T(4,128)(2,1)}), bf16[512,3,1024]{0,1,2:T(4,128)(2,1)}, u32[]{:S(2)}, u32[]{:S(2)}) async-start(bf16[512,3,1024]{0,1,2:T(4,128)(2,1)} %copy.29), calls=%async_computation | async-start | bytes 8388608 | tf_op jit(solution)/shard_map/all_to_all | solution.py:55
  33.3 133.8 %all-gather.5.cloned.1.call-start = ((), (), s32[]{:S(2)}) async-start(), calls=%async_computation.3 | async-start | bytes 2621440 | tf_op jit(solution)/shard_map/all_gather | solution.py:70
  107.8 38.9 %copy-start.9 = (s32[8]{0:T(128)S(1)}, s32[8]{0:T(128)}, u32[]{:S(2)}) copy-start(s32[8]{0:T(128)} %param.15) | copy-start | bytes 100
  107.8 4.1 %copy-start.4 = (bf16[2048,4,64]{0,2,1:T(8,128)(2,1)S(1)}, bf16[2048,4,64]{0,2,1:T(8,128)(2,1)}, u32[]{:S(2)}) copy-start(bf16[2048,4,64]{0,2,1:T(8,128)(2,1)} %get-tuple-element.136) | copy-start | bytes 3145732 | tf_op jit(solution)/shard_map/while
  116.2 4.1 %copy-start.4 = (bf16[2048,4,64]{0,2,1:T(8,128)(2,1)S(1)}, bf16[2048,4,64]{0,2,1:T(8,128)(2,1)}, u32[]{:S(2)}) copy-start(bf16[2048,4,64]{0,2,1:T(8,128)(2,1)} %get-tuple-element.136) | copy-start | bytes 3145732 | tf_op jit(solution)/shard_map/while
  124.6 4.0 %copy-start.4 = (bf16[2048,4,64]{0,2,1:T(8,128)(2,1)S(1)}, bf16[2048,4,64]{0,2,1:T(8,128)(2,1)}, u32[]{:S(2)}) copy-start(bf16[2048,4,64]{0,2,1:T(8,128)(2,1)} %get-tuple-element.136) | copy-start | bytes 3145732 | tf_op jit(solution)/shard_map/while
  132.9 4.0 %copy-start.4 = (bf16[2048,4,64]{0,2,1:T(8,128)(2,1)S(1)}, bf16[2048,4,64]{0,2,1:T(8,128)(2,1)}, u32[]{:S(2)}) copy-start(bf16[2048,4,64]{0,2,1:T(8,128)(2,1)} %get-tuple-element.136) | copy-start | bytes 3145732 | tf_op jit(solution)/shard_map/while
  141.3 18.0 %all-to-all-start.1 = ((bf16[4,512,256]{1,2,0:T(8,128)(2,1)}), bf16[4,512,256]{1,2,0:T(8,128)(2,1)S(1)}, u32[]{:S(2)}, u32[]{:S(2)}) async-start(bf16[4,512,256]{1,2,0:T(8,128)(2,1)} %bitcast.80), calls=%async_computation.1 | async-start | bytes 2097152 | tf_op jit(solution)/shard_map/all_to_all | solution.py:60
  159.2 4.1 %copy-start.5 = (bf16[1024,1024]{1,0:T(8,128)(2,1)S(1)}, bf16[1024,1024]{1,0:T(8,128)(2,1)}, u32[]{:S(2)}) copy-start(bf16[1024,1024]{1,0:T(8,128)(2,1)} %param.21) | copy-start | bytes 6291460
  159.2 4.1 %copy-start.7 = (f32[1024]{0:T(1024)S(1)}, f32[1024]{0:T(1024)}, u32[]{:S(2)}) copy-start(f32[1024]{0:T(1024)} %param.20) | copy-start | bytes 12292
  162.0 1.3 copy-start.1
  171.0 5.5 %copy-start.3 = (bf16[512,2048]{0,1:T(8,128)(2,1)S(1)}, bf16[512,2048]{0,1:T(8,128)(2,1)}, u32[]{:S(2)}) copy-start(bf16[512,2048]{0,1:T(8,128)(2,1)} %copy.33) | copy-start | bytes 6291460
  176.6 3.8 %copy-start.2 = (f32[512,1024]{1,0:T(8,128)S(1)}, f32[512,1024]{1,0:T(8,128)}, u32[]{:S(2)}) copy-start(f32[512,1024]{1,0:T(8,128)} %copy-done.1) | copy-start | bytes 6291460
  176.6 3.8 %copy-start.6 = (bf16[1024,1024]{1,0:T(8,128)(2,1)S(1)}, bf16[1024,1024]{1,0:T(8,128)(2,1)}, u32[]{:S(2)}) copy-start(bf16[1024,1024]{1,0:T(8,128)(2,1)} %param.23) | copy-start | bytes 6291460
Sparse Core Ops, SparseCore 0:
  9.5 51.9 all-gather.2
  107.9 23.6 all-gather.4
where the time goes:
time: 190 us; the launch traced here: 189 us
  matrix products  62 us (33%)
  waiting for transfers between devices  58.4 us (31%)
  local copies, waits for them, and re-layouts  41 us (22%)
  between operations  16.9 us (9%)
  starting transfers between devices  8.93 us (5%)
  other arithmetic  2.16 us (1%)
    all_to_all x1, waiting for transfers between devices, per_device(): lax.all_to_all(stacked, 'seq', split_axis=2, concat_axis=0, tiled=True)  46.4 us
    dot_general x5, matrix products, one_block(): jnp.einsum('qhd,khd->hqk', query_block, keys, preferred_element_type=jnp....  21.7 us
    dot_general x5, matrix products, one_block(): jnp.einsum('hqk,khd->qhd', weights, values, preferred_element_type=jnp.fl...  20.9 us
    all_to_all x1, waiting for transfers between devices, per_device(): lax.all_to_all(attended, 'seq', split_axis=0, concat_axis=1, tiled=True)  11.3 us
    dot_general x1, matrix products, per_device(): jnp.dot(normed, w_qkv, preferred_element_type=jnp.float32)  8.28 us
    all_to_all x2, local copies, waits for them, and re-layouts, per_device(): lax.all_to_all(stacked, 'seq', split_axis=2, concat_axis=0, tiled=True)  7.07 us
    reshape x1, local copies, waits for them, and re-layouts, per_device(): stacked = projected.reshape(tok_rows, 3, D)  6.53 us
    reshape x1, local copies, waits for them, and re-layouts, per_device(): split = local_heads.reshape(seq_rows, 3, head_count, HEAD_DIM)  6.1 us
  transfers between devices with their start and end apart: 4, of which 2 were waited for; matrix products, arithmetic and copies ran while one was open for 45% of the time, Pallas kernels for 0%

commit v1 on v0

--- a/solution.py
+++ b/solution.py
@@ -6,6 +6,28 @@
 D = 1024
 HEADS = 16
 HEAD_DIM = 64
+
+
+def laid_out(blocks, dim):
+    lengths = list(blocks.shape[1:])
+    lengths[dim] *= blocks.shape[0]
+    return jnp.moveaxis(blocks, 0, dim).reshape(lengths)
+
+
+def gather_around(array, axis, dim):
+    count = lax.axis_size(axis)
+    pairs = [(i, (i + 1) % count) for i in range(count)]
+    back = [(b, a) for a, b in pairs]
+    lower, upper = ([], [])
+    for step in range(count - 1):
+        if step % 2 == 0:
+            lower.append(lax.ppermute(lower[-1] if lower else array, axis, pairs))
+        else:
+            upper.append(lax.ppermute(upper[-1] if upper else array, axis, back))
+    blocks = jnp.stack([*lower[::-1], array, *upper])
+    shift = lax.axis_index(axis) - len(lower)
+    blocks = blocks[(jnp.arange(count) - shift) % count]
+    return laid_out(blocks, dim)
 
 
 def normalize(values, gain):
@@ -67,7 +89,7 @@
     empty = jnp.zeros(eq_embed.shape[1:], jnp.bfloat16)
     owned_rows = pick_slot(slot, empty, lax.all_gather(eq_embed, "dp", axis=0, tiled=True))
     owned_kv = jnp.dot(owned_rows, w_ckv, preferred_element_type=jnp.float32).astype(jnp.bfloat16)
-    whole_kv = lax.all_gather(owned_kv, "seq", axis=0, tiled=True)
+    whole_kv = gather_around(owned_kv, "seq", 0)
     whole_kv = whole_kv.reshape(eq_rows * groups, 2, HEADS, HEAD_DIM)
     valid = jnp.arange(eq_rows * groups, dtype=jnp.int32) < length
     cross_att = attend(

time: 190 us -> 207 us (1.089)
  local copies, waits for them, and re-layouts: 41 us -> 47.9 us
  waiting for transfers between devices: 58.4 us -> 63.1 us
  other arithmetic: 2.16 us -> 5.48 us
    ppermute x0 -> x3, waiting for transfers between devices: none -> 10 us  [the longest x2 5.75 us: gather_around(): lower.append(lax.ppermute(lower[-1] if lower else array, axis, pairs))]
    gather x0 -> x2, local copies, waits for them, and re-layouts: none -> 7.85 us  [gather_around(): blocks = blocks[(jnp.arange(count) - shift) % count]]
    all_to_all x1, waiting for transfers between devices: 11.3 us -> 4.39 us  [per_device(): lax.all_to_all(attended, 'seq', split_axis=0, concat_axis=1, tiled=True)]
    another operation x0 -> x1, local copies, waits for them, and re-layouts: none -> 4.13 us  [per_device(): whole_kv = whole_kv.reshape(eq_rows * groups, 2, HEADS, HEAD_DIM)]
    all_gather x1 -> x0, local copies, waits for them, and re-layouts: 3.93 us -> none  [per_device(): whole_kv = lax.all_gather(owned_kv, 'seq', axis=0, tiled=True)]
    another operation x0 -> x1, other arithmetic: none -> 3.1 us  [gather_around(): blocks = jnp.stack([*lower[::-1], array, *upper])]
  transfers between devices with their start and end apart: 4 -> 6, of which waited for: 2 -> 5; matrix products, arithmetic and copies ran while one was open for 45% -> 33% of each run, Pallas kernels for 0% -> 0%
where the time goes in v1:
time: 207 us; the launch traced here: 206 us
  waiting for transfers between devices  63.1 us (30%)
  matrix products  62 us (30%)
  local copies, waits for them, and re-layouts  47.9 us (23%)
  between operations  17.7 us (9%)
  starting transfers between devices  9.95 us (5%)
  other arithmetic  5.48 us (3%)
    all_to_all x1, waiting for transfers between devices, per_device(): lax.all_to_all(stacked, 'seq', split_axis=2, concat_axis=0, tiled=True)  48.2 us
    dot_general x5, matrix products, one_block(): jnp.einsum('qhd,khd->hqk', query_block, keys, preferred_element_type=jnp....  21.6 us
    dot_general x5, matrix products, one_block(): jnp.einsum('hqk,khd->qhd', weights, values, preferred_element_type=jnp.fl...  20.9 us
    dot_general x1, matrix products, per_device(): jnp.dot(normed, w_qkv, preferred_element_type=jnp.float32)  8.28 us
    gather x2, local copies, waits for them, and re-layouts, gather_around(): blocks = blocks[(jnp.arange(count) - shift) % count]  7.85 us
    all_to_all x2, local copies, waits for them, and re-layouts, per_device(): lax.all_to_all(stacked, 'seq', split_axis=2, concat_axis=0, tiled=True)  7.08 us
    reshape x1, local copies, waits for them, and re-layouts, per_device(): stacked = projected.reshape(tok_rows, 3, D)  6.53 us
    reshape x1, local copies, waits for them, and re-layouts, per_device(): split = local_heads.reshape(seq_rows, 3, head_count, HEAD_DIM)  6.1 us
  transfers between devices with their start and end apart: 6, of which 5 were waited for; matrix products, arithmetic and copies ran while one was open for 33% of the time, Pallas kernels for 0%

profile of v1, /device:TPU:0, one launch (start us, length us, event | category | flops | bytes accessed | tf_op | source)
XLA Modules:
  0.0 206.2 jit_solution(17085178562978198239)
XLA Ops:
  6.5 1.7 fusion.12
  8.2 8.3 %convolution_convert_fusion = bf16[512,3072]{1,0:T(8,128)(2,1)} fusion(bf16[1024,3072]{1,0:T(8,128)(2,1)} %param.18, bf16[1,512,1024]{2,1,0:T(8,128)(2,1)} %param.13, f32[1024]{0:T(1024)} %param.17, f32[512]{0:T(512)S(1)} %add_rsqrt_fusion.1), kind=kOutput, calls=%fused_computation.17 | convolution fusion | flops 3224895488 | bytes 10491904 | tf_op jit(solution)/shard_map/dot_general | solution.py:75
  16.5 4.7 %copy.28 = bf16[512,3072]{0,1:T(8,128)(2,1)} copy(bf16[512,3072]{1,0:T(8,128)(2,1)} %convolution_convert_fusion) | data formatting | bytes 6291456 | tf_op jit(solution)/shard_map/convert_element_type | solution.py:75
  21.1 6.5 %copy.29 = bf16[512,3,1024]{0,1,2:T(4,128)(2,1)} copy(bf16[512,3,1024]{0,2,1:T(8,128)(2,1)} %bitcast.82) | data formatting | bytes 6291456 | tf_op jit(solution)/shard_map/reshape | solution.py:76
  27.7 4.8 %all-to-all-start = ((bf16[512,3,1024]{0,1,2:T(4,128)(2,1)}), bf16[512,3,1024]{0,1,2:T(4,128)(2,1)}, u32[]{:S(2)}, u32[]{:S(2)}) async-start(bf16[512,3,1024]{0,1,2:T(4,128)(2,1)} %copy.29), calls=%async_computation | async-start | bytes 8388608 | tf_op jit(solution)/shard_map/all_to_all | solution.py:77
  32.5 0.2 all-gather.2.cloned.1.call-start
  32.8 0.5 all-gather.2.cloned.1.call-update
  33.3 48.2 %all-to-all-done = bf16[512,3,1024]{0,1,2:T(4,128)(2,1)} async-done(((bf16[512,3,1024]{0,1,2:T(4,128)(2,1)}), bf16[512,3,1024]{0,1,2:T(4,128)(2,1)}, u32[]{:S(2)}, u32[]{:S(2)}) %all-to-all-start) | async-done | bytes 3145760 | tf_op jit(solution)/shard_map/all_to_all | solution.py:77
  81.4 3.0 %copy.30 = bf16[512,3,1024]{0,2,1:T(8,128)(2,1)S(1)} copy(bf16[512,3,1024]{0,1,2:T(4,128)(2,1)} %all-to-all-done) | data formatting | bytes 6291456 | tf_op jit(solution)/shard_map/all_to_all | solution.py:77
  84.4 4.1 %copy.31 = bf16[4,512,3,256]{1,0,3,2:T(4,128)(2,1)} copy(bf16[4,512,3,256]{1,3,0,2:T(8,128)(2,1)S(1)} %bitcast.83) | data formatting | bytes 6291456 | tf_op jit(solution)/shard_map/all_to_all | solution.py:77
  88.5 6.1 %reshape.96 = bf16[2048,3,4,64]{0,3,2,1:T(8,128)(2,1)} reshape(bf16[4,512,3,256]{1,0,3,2:T(4,128)(2,1)} %copy.31) | data formatting | bytes 6291456 | tf_op jit(solution)/shard_map/reshape | solution.py:79
  94.6 3.6 %slice_bitcast_fusion.4 = (bf16[2048,4,64]{0,2,1:T(8,128)(2,1)}, bf16[2048,4,64]{0,2,1:T(8,128)(2,1)S(1)}, bf16[2048,1,4,64]{0,3,2,1:T(8,128)(2,1)}) fusion(bf16[2048,3,4,64]{0,3,2,1:T(8,128)(2,1)} %reshape.96), kind=kLoop, calls=%fused_computation.35 | loop fusion | bytes 6291456 | tf_op jit(solution)/shard_map/squeeze | solution.py:81
  98.2 2.6 %reshape_squeeze.3 = bf16[4,512,4,64]{1,0,3,2:T(4,128)(2,1)} reshape(bf16[2048,1,4,64]{0,3,2,1:T(8,128)(2,1)} %get-tuple-element.80) | data formatting | bytes 2097152 | tf_op jit(solution)/shard_map/reshape;squeeze | solution.py:55
  100.8 2.4 %copy.32 = bf16[4,512,4,64]{1,3,2,0:T(8,128)(2,1)} copy(bf16[4,512,4,64]{1,0,3,2:T(4,128)(2,1)} %reshape_squeeze.3) | data formatting | bytes 2097152 | tf_op jit(solution)/shard_map/while | solution.py:55
  103.2 33.4 %while.2 = (s32[]{:T(128)}, bf16[4,512,4,64]{1,3,2,0:T(8,128)(2,1)}, bf16[4,512,4,64]{1,3,2,0:T(8,128)(2,1)}, bf16[2048,4,64]{0,2,1:T(8,128)(2,1)S(1)}, bf16[2048,4,64]{0,2,1:T(8,128)(2,1)}, /*index=5*/s32[]{:T(128)}) while((s32[]{:T(128)}, bf16[4,512,4,64]{1,3,2,0:T(8,128)(2,1)}, bf16[4,512,4,64]{1,3,2,0:T(8,128)(2,1)}, ...), condition=%wide.region_3.4_spmd, body=%wide.region_1.3_spmd.sunk | while | flops 1094842368 | bytes 40386672 | solution.py:55
  103.3 4.0 %fusion.51 = (f32[4,512]{1,0:T(4,128)S(1)}, f32[4,512,2048]{2,1,0:T(8,128)S(1)}) fusion(bf16[2048,4,64]{0,2,1:T(8,128)(2,1)S(1)} %get-tuple-element.135, bf16[4,512,4,64]{1,3,2,0:T(8,128)(2,1)} %get-tuple-element.134, s32[]{:T(128)S(6)} %copy.40), kind=kOutput, calls=%fused_computation.3.clone.1 | convolution fusion | flops 545257472 | bytes 18096132 | tf_op jit(solution)/shard_map/while/body/eval_jaxpr/qhd,khd->hqk/dot_general | solution.py:46
  107.3 4.3 %fusion.52 = bf16[4,512,4,64]{1,3,2,0:T(8,128)(2,1)} fusion(bf16[4,512,4,64]{1,3,2,0:T(8,128)(2,1)} %get-tuple-element.127, s32[]{:T(128)S(6)} %copy.40, bf16[2048,4,64]{0,2,1:T(8,128)(2,1)S(1)} %copy-done.5, f32[4,512,2048]{2,1,0:T(8,128)S(1)} %get-tuple-element.118, f32[4,512]{1,0:T(4,128)S(1)} %get-tuple-element.119), kind=kOutput, calls=%fused_computation.7.clone.1 | convolution fusion | flops 549584896 | bytes 18096132 | tf_op jit(solution)/shard_map/while/body/eval_jaxpr/hqk,khd->qhd/dot_general | solution.py:51
  111.6 4.0 %fusion.51 = (f32[4,512]{1,0:T(4,128)S(1)}, f32[4,512,2048]{2,1,0:T(8,128)S(1)}) fusion(bf16[2048,4,64]{0,2,1:T(8,128)(2,1)S(1)} %get-tuple-element.135, bf16[4,512,4,64]{1,3,2,0:T(8,128)(2,1)} %get-tuple-element.134, s32[]{:T(128)S(6)} %copy.40), kind=kOutput, calls=%fused_computation.3.clone.1 | convolution fusion | flops 545257472 | bytes 18096132 | tf_op jit(solution)/shard_map/while/body/eval_jaxpr/qhd,khd->hqk/dot_general | solution.py:46
  115.6 4.3 %fusion.52 = bf16[4,512,4,64]{1,3,2,0:T(8,128)(2,1)} fusion(bf16[4,512,4,64]{1,3,2,0:T(8,128)(2,1)} %get-tuple-element.127, s32[]{:T(128)S(6)} %copy.40, bf16[2048,4,64]{0,2,1:T(8,128)(2,1)S(1)} %copy-done.5, f32[4,512,2048]{2,1,0:T(8,128)S(1)} %get-tuple-element.118, f32[4,512]{1,0:T(4,128)S(1)} %get-tuple-element.119), kind=kOutput, calls=%fused_computation.7.clone.1 | convolution fusion | flops 549584896 | bytes 18096132 | tf_op jit(solution)/shard_map/while/body/eval_jaxpr/hqk,khd->qhd/dot_general | solution.py:51
  120.0 4.0 %fusion.51 = (f32[4,512]{1,0:T(4,128)S(1)}, f32[4,512,2048]{2,1,0:T(8,128)S(1)}) fusion(bf16[2048,4,64]{0,2,1:T(8,128)(2,1)S(1)} %get-tuple-element.135, bf16[4,512,4,64]{1,3,2,0:T(8,128)(2,1)} %get-tuple-element.134, s32[]{:T(128)S(6)} %copy.40), kind=kOutput, calls=%fused_computation.3.clone.1 | convolution fusion | flops 545257472 | bytes 18096132 | tf_op jit(solution)/shard_map/while/body/eval_jaxpr/qhd,khd->hqk/dot_general | solution.py:46
  124.0 4.3 %fusion.52 = bf16[4,512,4,64]{1,3,2,0:T(8,128)(2,1)} fusion(bf16[4,512,4,64]{1,3,2,0:T(8,128)(2,1)} %get-tuple-element.127, s32[]{:T(128)S(6)} %copy.40, bf16[2048,4,64]{0,2,1:T(8,128)(2,1)S(1)} %copy-done.5, f32[4,512,2048]{2,1,0:T(8,128)S(1)} %get-tuple-element.118, f32[4,512]{1,0:T(4,128)S(1)} %get-tuple-element.119), kind=kOutput, calls=%fused_computation.7.clone.1 | convolution fusion | flops 549584896 | bytes 18096132 | tf_op jit(solution)/shard_map/while/body/eval_jaxpr/hqk,khd->qhd/dot_general | solution.py:51
  128.3 4.0 %fusion.51 = (f32[4,512]{1,0:T(4,128)S(1)}, f32[4,512,2048]{2,1,0:T(8,128)S(1)}) fusion(bf16[2048,4,64]{0,2,1:T(8,128)(2,1)S(1)} %get-tuple-element.135, bf16[4,512,4,64]{1,3,2,0:T(8,128)(2,1)} %get-tuple-element.134, s32[]{:T(128)S(6)} %copy.40), kind=kOutput, calls=%fused_computation.3.clone.1 | convolution fusion | flops 545257472 | bytes 18096132 | tf_op jit(solution)/shard_map/while/body/eval_jaxpr/qhd,khd->hqk/dot_general | solution.py:46
  132.4 4.3 %fusion.52 = bf16[4,512,4,64]{1,3,2,0:T(8,128)(2,1)} fusion(bf16[4,512,4,64]{1,3,2,0:T(8,128)(2,1)} %get-tuple-element.127, s32[]{:T(128)S(6)} %copy.40, bf16[2048,4,64]{0,2,1:T(8,128)(2,1)S(1)} %copy-done.5, f32[4,512,2048]{2,1,0:T(8,128)S(1)} %get-tuple-element.118, f32[4,512]{1,0:T(4,128)S(1)} %get-tuple-element.119), kind=kOutput, calls=%fused_computation.7.clone.1 | convolution fusion | flops 549584896 | bytes 18096132 | tf_op jit(solution)/shard_map/while/body/eval_jaxpr/hqk,khd->qhd/dot_general | solution.py:51
  136.7 4.4 %all-to-all-start.1 = ((bf16[4,512,256]{1,2,0:T(8,128)(2,1)}), bf16[4,512,256]{1,2,0:T(8,128)(2,1)}, u32[]{:S(2)}, u32[]{:S(2)}) async-start(bf16[4,512,256]{1,2,0:T(8,128)(2,1)} %bitcast.84), calls=%async_computation.1 | async-start | bytes 2097152 | tf_op jit(solution)/shard_map/all_to_all | solution.py:82
  141.1 0.7 dynamic_slice.18
  145.9 0.7 dynamic_slice.20
  146.6 0.0 copy-start.1
  146.6 0.0 all-gather.2.cloned.1.call-done
  146.6 3.9 %convolution_convert_fusion.1 = bf16[128,2048]{1,0:T(8,128)(2,1)} fusion(bf16[1024,2048]{1,0:T(8,128)(2,1)} %param.22, bf16[8,128,1024]{2,1,0:T(8,128)(2,1)} %all-gather.2.cloned.1.call-done, s32[]{:T(128)S(6)} %min.4, pred[]{:T(512)S(6)} %and.23), kind=kOutput, calls=%fused_computation.21 | convolution fusion | flops 537264128 | bytes 4980741 | tf_op jit(solution)/shard_map/dot_general | solution.py:91
  150.5 0.4 collective-permute-start
  150.9 0.7 iota_compare_fusion
  151.6 4.4 %all-to-all-done.1 = bf16[4,512,256]{1,2,0:T(8,128)(2,1)} async-done(((bf16[4,512,256]{1,2,0:T(8,128)(2,1)}), bf16[4,512,256]{1,2,0:T(8,128)(2,1)}, u32[]{:S(2)}, u32[]{:S(2)}) %all-to-all-start.1) | async-done | bytes 1048608 | tf_op jit(solution)/shard_map/all_to_all | solution.py:82
  156.1 2.7 %multiply_reduce_fusion = (f32[512]{0:T(512)S(1)}, f32[512,1024]{1,0:T(8,128)S(1)}) fusion(bf16[512,1024]{0,1:T(8,128)(2,1)} %bitcast.12, bf16[1024,1024]{1,0:T(8,128)(2,1)S(1)} %copy-done, bf16[1,512,1024]{2,1,0:T(8,128)(2,1)S(1)} %copy-done.1), kind=kOutput, calls=%fused_computation.28 | convolution fusion | flops 1075838464 | bytes 6293504 | tf_op jit(solution)/shard_map/dot_general | solution.py:83
  158.8 0.1 collective-permute-start.2
  158.9 2.3 %collective-permute-done = bf16[128,2048]{1,0:T(8,128)(2,1)} collective-permute-done((bf16[128,2048]{1,0:T(8,128)(2,1)}, bf16[128,2048]{1,0:T(8,128)(2,1)}, u32[]{:S(2)}, u32[]{:S(2)}) %collective-permute-start) | collective-permute-done | bytes 524320 | tf_op jit(solution)/shard_map/ppermute | solution.py:24
  161.2 0.0 collective-permute-start.1
  161.2 2.3 %convolution_convert_fusion.2 = bf16[512,1024]{1,0:T(8,128)(2,1)} fusion(bf16[1024,1024]{1,0:T(8,128)(2,1)S(1)} %copy-done.6, f32[512,1024]{1,0:T(8,128)S(1)} %get-tuple-element.82, f32[1024]{0:T(1024)S(1)} %copy-done.8, f32[512]{0:T(512)S(1)} %add_rsqrt_fusion), kind=kOutput, calls=%fused_computation.30 | convolution fusion | flops 1075838976 | bytes 5249024 | tf_op jit(solution)/shard_map/dot_general | solution.py:85
  163.5 1.5 copy.34
  165.0 4.3 %collective-permute-done.2 = bf16[128,2048]{1,0:T(8,128)(2,1)} collective-permute-done((bf16[128,2048]{1,0:T(8,128)(2,1)}, bf16[128,2048]{1,0:T(8,128)(2,1)}, u32[]{:S(2)}, u32[]{:S(2)}) %collective-permute-start.2) | collective-permute-done | bytes 524320 | tf_op jit(solution)/shard_map/ppermute | solution.py:26
  169.3 3.4 %collective-permute-done.1 = bf16[128,2048]{1,0:T(8,128)(2,1)} collective-permute-done((bf16[128,2048]{1,0:T(8,128)(2,1)}, bf16[128,2048]{1,0:T(8,128)(2,1)}, u32[]{:S(2)}, u32[]{:S(2)}) %collective-permute-start.1) | collective-permute-done | bytes 524320 | tf_op jit(solution)/shard_map/ppermute | solution.py:24
  172.7 3.1 %pad_maximum_fusion = bf16[4,128,2048]{2,1,0:T(8,128)(2,1)} fusion(bf16[1,128,2048]{2,1,0:T(8,128)(2,1)} %bitcast.18, bf16[1,128,2048]{2,1,0:T(8,128)(2,1)} %bitcast.17, bf16[1,128,2048]{2,1,0:T(8,128)(2,1)} %bitcast.16, bf16[1,128,2048]{2,1,0:T(8,128)(2,1)} %bitcast.15), kind=kLoop, calls=%fused_computation.25 | loop fusion | flops 3145728 | bytes 4194304 | tf_op jit(solution)/shard_map/stack | solution.py:27
  175.8 3.6 %gather_fusion = bf16[4,128,2048]{2,1,0:T(8,128)(2,1)} fusion(bf16[4,128,2048]{2,1,0:T(8,128)(2,1)} %pad_maximum_fusion, s32[1024]{0:T(1024)S(1)} %pad_clamp_fusion), kind=kCustom, calls=%fused_computation | custom fusion | bytes 4194320 | tf_op jit(solution)/shard_map/gather | solution.py:29
  179.4 4.2 %copy.33 = bf16[4,128,2048]{1,0,2:T(4,128)(2,1)} copy(bf16[4,128,2048]{2,1,0:T(8,128)(2,1)} %gather_fusion) | data formatting | bytes 4194304 | tf_op jit(solution)/shard_map/gather | solution.py:29
  183.7 4.1 %reshape_reshape.4 = bf16[512,2,16,64]{0,3,2,1:T(8,128)(2,1)} reshape(bf16[4,128,2048]{1,0,2:T(4,128)(2,1)} %copy.33) | data formatting | bytes 4194304 | tf_op jit(solution)/shard_map/reshape;reshape | solution.py:93
  187.8 5.5 %fusion.10 = (f32[16,512]{1,0:T(8,128)S(1)}, f32[16,512,512]{1,2,0:T(8,128)S(1)}) fusion(pred[512]{0:T(512)(128)(4,1)S(1)} %iota_compare_fusion, bf16[512,16,64]{0,2,1:T(8,128)(2,1)S(1)} %bitcast.85, bf16[512,2,16,64]{0,3,2,1:T(8,128)(2,1)} %reshape_reshape.4), kind=kOutput, calls=%fused_computation.15 | convolution fusion | flops 549445632 | bytes 18907648 | tf_op jit(solution)/shard_map/while/body/eval_jaxpr/qhd,khd->hqk/dot_general | solution.py:46
  193.4 0.0 copy-start.7
  193.4 3.7 %fusion.15 = bf16[16,64,512]{2,1,0:T(8,128)(2,1)S(1)} fusion(f32[16,512,512]{1,2,0:T(8,128)S(1)} %get-tuple-element.84, f32[16,512]{1,0:T(8,128)S(1)} %get-tuple-element.83, pred[512]{0:T(512)(128)(4,1)S(1)} %iota_compare_fusion, bf16[512,2,16,64]{0,3,2,1:T(8,128)(2,1)S(1)} %copy-done.4), kind=kOutput, calls=%fused_computation.29 | convolution fusion | flops 554172416 | bytes 18907648 | tf_op jit(solution)/shard_map/while/body/eval_jaxpr/hqk,khd->qhd/dot_general | solution.py:51
  197.1 2.2 %fusion.16 = bf16[1,512,1024]{2,1,0:T(8,128)(2,1)} fusion(f32[512,1024]{1,0:T(8,128)S(1)} %copy-done.3, bf16[512,1024]{0,1:T(8,128)(2,1)S(1)} %bitcast.86, bf16[1024,1024]{1,0:T(8,128)(2,1)S(1)} %copy-done.7), kind=kOutput, calls=%fused_computation.31 | convolution fusion | flops 1074790400 | bytes 6291456 | tf_op jit(solution)/shard_map/dot_general | solution.py:98
  (31 shorter events, 0.1 us)
Async XLA Ops:
  6.5 149.5 %copy-start = (bf16[1024,1024]{1,0:T(8,128)(2,1)S(1)}, bf16[1024,1024]{1,0:T(8,128)(2,1)}, u32[]{:S(2)}) copy-start(bf16[1024,1024]{1,0:T(8,128)(2,1)} %param.19) | copy-start | bytes 6291460
  27.7 53.8 %all-to-all-start = ((bf16[512,3,1024]{0,1,2:T(4,128)(2,1)}), bf16[512,3,1024]{0,1,2:T(4,128)(2,1)}, u32[]{:S(2)}, u32[]{:S(2)}) async-start(bf16[512,3,1024]{0,1,2:T(4,128)(2,1)} %copy.29), calls=%async_computation | async-start | bytes 8388608 | tf_op jit(solution)/shard_map/all_to_all | solution.py:77
  32.5 114.1 %all-gather.2.cloned.1.call-start = ((), (), s32[]{:S(2)}) async-start(), calls=%async_computation.2 | async-start | bytes 2359296 | tf_op jit(solution)/shard_map/all_gather | solution.py:90
  103.2 4.0 %copy-start.5 = (bf16[2048,4,64]{0,2,1:T(8,128)(2,1)S(1)}, bf16[2048,4,64]{0,2,1:T(8,128)(2,1)}, u32[]{:S(2)}) copy-start(bf16[2048,4,64]{0,2,1:T(8,128)(2,1)} %get-tuple-element.136) | copy-start | bytes 3145732 | tf_op jit(solution)/shard_map/while
  111.6 4.0 %copy-start.5 = (bf16[2048,4,64]{0,2,1:T(8,128)(2,1)S(1)}, bf16[2048,4,64]{0,2,1:T(8,128)(2,1)}, u32[]{:S(2)}) copy-start(bf16[2048,4,64]{0,2,1:T(8,128)(2,1)} %get-tuple-element.136) | copy-start | bytes 3145732 | tf_op jit(solution)/shard_map/while
  119.9 4.0 %copy-start.5 = (bf16[2048,4,64]{0,2,1:T(8,128)(2,1)S(1)}, bf16[2048,4,64]{0,2,1:T(8,128)(2,1)}, u32[]{:S(2)}) copy-start(bf16[2048,4,64]{0,2,1:T(8,128)(2,1)} %get-tuple-element.136) | copy-start | bytes 3145732 | tf_op jit(solution)/shard_map/while
  128.3 4.0 %copy-start.5 = (bf16[2048,4,64]{0,2,1:T(8,128)(2,1)S(1)}, bf16[2048,4,64]{0,2,1:T(8,128)(2,1)}, u32[]{:S(2)}) copy-start(bf16[2048,4,64]{0,2,1:T(8,128)(2,1)} %get-tuple-element.136) | copy-start | bytes 3145732 | tf_op jit(solution)/shard_map/while
  136.7 4.4 %copy-start.9 = (s32[8]{0:T(128)S(1)}, s32[8]{0:T(128)}, u32[]{:S(2)}) copy-start(s32[8]{0:T(128)} %param.16) | copy-start | bytes 100
  136.7 9.2 %copy-start.10 = (s32[8]{0:T(128)S(1)}, s32[8]{0:T(128)}, u32[]{:S(2)}) copy-start(s32[8]{0:T(128)} %param.15) | copy-start | bytes 100
  136.7 19.4 %all-to-all-start.1 = ((bf16[4,512,256]{1,2,0:T(8,128)(2,1)}), bf16[4,512,256]{1,2,0:T(8,128)(2,1)}, u32[]{:S(2)}, u32[]{:S(2)}) async-start(bf16[4,512,256]{1,2,0:T(8,128)(2,1)} %bitcast.84), calls=%async_computation.1 | async-start | bytes 2097152 | tf_op jit(solution)/shard_map/all_to_all | solution.py:82
  146.6 9.5 %copy-start.1 = (bf16[1,512,1024]{2,1,0:T(8,128)(2,1)S(1)}, bf16[1,512,1024]{2,1,0:T(8,128)(2,1)}, u32[]{:S(2)}) copy-start(bf16[1,512,1024]{2,1,0:T(8,128)(2,1)} %param.13) | copy-start | bytes 3145732
  150.5 10.7 %collective-permute-start = (bf16[128,2048]{1,0:T(8,128)(2,1)}, bf16[128,2048]{1,0:T(8,128)(2,1)}, u32[]{:S(2)}, u32[]{:S(2)}) collective-permute-start(bf16[128,2048]{1,0:T(8,128)(2,1)} %convolution_convert_fusion.1), channel_id=1, source_target_pairs={{0,1},{1,2},{2,3},{3,0},{4,5},{5,6},{6,7},{7,4},{8,9},{9,10},{10,1... | collective-permute-start | bytes 1572872 | tf_op jit(solution)/shard_map/ppermute | solution.py:24
  156.0 5.2 %copy-start.6 = (bf16[1024,1024]{1,0:T(8,128)(2,1)S(1)}, bf16[1024,1024]{1,0:T(8,128)(2,1)}, u32[]{:S(2)}) copy-start(bf16[1024,1024]{1,0:T(8,128)(2,1)} %param.21) | copy-start | bytes 6291460
  156.0 5.2 %copy-start.8 = (f32[1024]{0:T(1024)S(1)}, f32[1024]{0:T(1024)}, u32[]{:S(2)}) copy-start(f32[1024]{0:T(1024)} %param.20) | copy-start | bytes 12292
  158.8 2.4 %copy-start.2 = (f32[512,1024]{1,0:T(8,128)}, f32[512,1024]{1,0:T(8,128)S(1)}, u32[]{:S(2)}) copy-start(f32[512,1024]{1,0:T(8,128)S(1)} %get-tuple-element.82) | copy-start | bytes 6291460
  158.8 10.5 %collective-permute-start.2 = (bf16[128,2048]{1,0:T(8,128)(2,1)}, bf16[128,2048]{1,0:T(8,128)(2,1)}, u32[]{:S(2)}, u32[]{:S(2)}) collective-permute-start(bf16[128,2048]{1,0:T(8,128)(2,1)} %convolution_convert_fusion.1), channel_id=1, source_target_pairs={{1,0},{2,1},{3,2},{0,3},{5,4},{6,5},{7,6},{4,7},{9,8},{10,9},{11,1... | collective-permute-start | bytes 1572872 | tf_op jit(solution)/shard_map/ppermute | solution.py:26
  161.2 11.5 %collective-permute-start.1 = (bf16[128,2048]{1,0:T(8,128)(2,1)}, bf16[128,2048]{1,0:T(8,128)(2,1)}, u32[]{:S(2)}, u32[]{:S(2)}) collective-permute-start(bf16[128,2048]{1,0:T(8,128)(2,1)} %collective-permute-done), channel_id=1, source_target_pairs={{0,1},{1,2},{2,3},{3,0},{4,5},{5,6},{6,7},{7,4},{8,9},{9,10},{10,1... | collective-permute-start | bytes 1572872 | tf_op jit(solution)/shard_map/ppermute | solution.py:24
  187.8 5.5 %copy-start.4 = (bf16[512,2,16,64]{0,3,2,1:T(8,128)(2,1)S(1)}, bf16[512,2,16,64]{0,3,2,1:T(8,128)(2,1)}, u32[]{:S(2)}) copy-start(bf16[512,2,16,64]{0,3,2,1:T(8,128)(2,1)} %reshape_reshape.4) | copy-start | bytes 6291460
  193.3 3.8 %copy-start.3 = (f32[512,1024]{1,0:T(8,128)S(1)}, f32[512,1024]{1,0:T(8,128)}, u32[]{:S(2)}) copy-start(f32[512,1024]{1,0:T(8,128)} %copy-done.2) | copy-start | bytes 6291460
  193.4 3.8 %copy-start.7 = (bf16[1024,1024]{1,0:T(8,128)(2,1)S(1)}, bf16[1024,1024]{1,0:T(8,128)(2,1)}, u32[]{:S(2)}) copy-start(bf16[1024,1024]{1,0:T(8,128)(2,1)} %param.23) | copy-start | bytes 6291460
Sparse Core Ops, SparseCore 0:
  35.5 52.4 all-gather.1
